TPU v7x, 32 devices: a whole 2x2x4 slice. The times are simulated.
32 devices in a mesh: group: 4 (over y, x), member: 8 (over z, core).
Axes of the slice: x: 2, y: 2, z: 4, core: 2. Of those that a mesh axis runs over, the one named last changes fastest.
Arguments:
- picture_embedding_matrix: bfloat16 [8192, 1152], P(('group', 'member')), may hold values from -1 to 1
- caption_embedding_matrix: bfloat16 [8192, 1152], P(('group', 'member')), may hold values from -1 to 1
- learned_sharpness: float32 [1], replicated, may hold values from 5 to 20
- learned_offset_entry: float32 [1], replicated, may hold values from -4 to -2
Outputs:
- grad_images: float32 [8192, 1152], P(('group', 'member'))
- grad_texts: float32 [8192, 1152], P(('group', 'member'))
All inputs are finite; a program needn't handle non-finite values.
Results may differ from a plain program's by a relative error of at most 0.002.
Values may be sent and summed in bfloat16 or wider, within the bound.
A program may use at most 192 MiB of HBM per device.

v0:
```python
import jax
import jax.numpy as jnp
from jax import lax
from jax.sharding import PartitionSpec as P


def passed_along(shard, axis, by):
    devices = lax.axis_size(axis)
    return lax.ppermute(shard, axis, [(i, (i + by) % devices) for i in range(devices)])


def weighting_factors(similarity_scores, match_polarity, sharpness_multiplier):
    return (
        -sharpness_multiplier * match_polarity * jax.nn.sigmoid(-match_polarity * similarity_scores)
    ).astype(jnp.bfloat16)


def shards(
    picture_embedding_matrix, caption_embedding_matrix, learned_sharpness, learned_offset_entry
):
    sharpness_multiplier = learned_sharpness[0]
    offset_amount = learned_offset_entry[0]
    count_of_rows = picture_embedding_matrix.shape[0]
    member_idx = lax.axis_index("member")
    members = lax.axis_size("member")
    columns = lax.broadcasted_iota(jnp.int32, (count_of_rows, count_of_rows * members), 1)
    targets = (
        lax.broadcasted_iota(jnp.int32, (count_of_rows, count_of_rows * members), 0)
        + member_idx * count_of_rows
    )
    match_polarity = jnp.where(columns == targets, 1.0, -1.0).astype(jnp.float32)
    txt_prev = passed_along(caption_embedding_matrix, "group", 1)
    earlier_scores = (
        sharpness_multiplier
        * jnp.dot(picture_embedding_matrix, txt_prev.T, preferred_element_type=jnp.float32)
        + offset_amount
    )
    earlier_multipliers = weighting_factors(earlier_scores, -1.0, sharpness_multiplier)
    grad_prev = jnp.dot(earlier_multipliers, txt_prev, preferred_element_type=jnp.float32)
    group_text_rows, group_img = (
        lax.all_gather(caption_embedding_matrix, "member", axis=0, tiled=True),
        lax.all_gather(picture_embedding_matrix, "member", axis=0, tiled=True),
    )
    similarity_scores = (
        sharpness_multiplier
        * jnp.dot(picture_embedding_matrix, group_text_rows.T, preferred_element_type=jnp.float32)
        + offset_amount
    )
    score_multipliers = weighting_factors(similarity_scores, match_polarity, sharpness_multiplier)
    grad_images = (
        jnp.dot(score_multipliers, group_text_rows, preferred_element_type=jnp.float32) + grad_prev
    )
    text_logits = (
        sharpness_multiplier
        * jnp.dot(caption_embedding_matrix, group_img.T, preferred_element_type=jnp.float32)
        + offset_amount
    )
    text_coeffs = weighting_factors(text_logits, match_polarity, sharpness_multiplier)
    img_next = passed_along(picture_embedding_matrix, "group", -1)
    next_logits = (
        sharpness_multiplier
        * jnp.dot(caption_embedding_matrix, img_next.T, preferred_element_type=jnp.float32)
        + offset_amount
    )
    next_coeffs = weighting_factors(next_logits, -1.0, sharpness_multiplier)
    grad_texts = jnp.dot(text_coeffs, group_img, preferred_element_type=jnp.float32)
    grad_texts = grad_texts + jnp.dot(next_coeffs, img_next, preferred_element_type=jnp.float32)
    return (grad_images, grad_texts)


def solution(mesh):
    in_specs = (P(("group", "member"), None), P(("group", "member"), None), P(), P())
    out_specs = (P(("group", "member"), None), P(("group", "member"), None))
    return jax.shard_map(shards, mesh=mesh, in_specs=in_specs, out_specs=out_specs, check_vma=False)
```

profile of v0, /device:TPU:0, one launch (start us, length us, event | category | flops | bytes accessed | tf_op | source)
XLA Modules:
  0.0 134.1 jit_solution(1650488425485670412)
XLA Ops:
  7.2 0.0 all-gather.5.cloned.1.call-start
  7.2 0.7 all-gather.5.cloned.1.call-update
  7.9 0.0 all-gather.3.cloned.1.call-start
  7.9 0.7 all-gather.3.cloned.1.call-update
  8.6 4.0 %collective-permute-start.1 = (bf16[256,1152]{1,0:T(8,128)(2,1)}, bf16[256,1152]{1,0:T(8,128)(2,1)S(1)}, u32[]{:S(2)}, u32[]{:S(2)}) collective-permute-start(bf16[256,1152]{1,0:T(8,128)(2,1)} %param.4), channel_id=1, source_target_pairs={{0,24},{8,0},{16,8},{24,16},{1,25},{9,1},{17,9},{25,17},{2,26},{10... | collective-permute-start | bytes 1769480 | tf_op jit(solution)/shard_map/ppermute | solution.py:9
  12.6 0.0 collective-permute-start
  13.9 49.6 %all-gather.5.cloned.1.call-done = bf16[2048,1152]{1,0:T(8,128)(2,1)} async-done(((bf16[256,1152]{1,0:T(8,128)(2,1)}), bf16[2048,1152]{1,0:T(8,128)(2,1)}) %all-gather.5.cloned.1.call-update) | async-done | bytes 4718608 | tf_op jit(solution)/shard_map/all_gather | solution.py:42
  63.6 0.0 copy-start.1
  63.6 8.1 %fusion.17 = f32[256,1152]{1,0:T(8,128)} fusion(bf16[2048,1152]{1,0:T(8,128)(2,1)} %all-gather.5.cloned.1.call-done, bf16[256,1152]{1,0:T(8,128)(2,1)} %param.5, f32[]{:T(128)} %bitcast.21, f32[]{:T(128)} %bitcast.17, s32[256]{0:T(256)S(1)} %iota_add_fusion, f32[]{:T(128)S(6)} %neg.22), kind=kOutput, calls=%fused_computation.24 | convolution fusion | flops 2422210560 | bytes 6489100 | tf_op jit(solution)/shard_map/dot_general | solution.py:66
  71.7 43.6 %all-gather.3.cloned.1.call-done = bf16[2048,1152]{1,0:T(8,128)(2,1)} async-done(((bf16[256,1152]{1,0:T(8,128)(2,1)}), bf16[2048,1152]{1,0:T(8,128)(2,1)}) %all-gather.3.cloned.1.call-update) | async-done | bytes 4718608 | tf_op jit(solution)/shard_map/all_gather | solution.py:41
  115.2 0.0 copy-done.1
  115.2 0.0 copy-start
  115.2 6.9 %fusion.16 = f32[256,1152]{1,0:T(8,128)S(1)} fusion(bf16[2048,1152]{1,0:T(8,128)(2,1)} %all-gather.3.cloned.1.call-done, bf16[256,1152]{1,0:T(8,128)(2,1)S(1)} %copy-done.1, f32[]{:T(128)} %bitcast.19, f32[]{:T(128)} %bitcast.15, s32[256]{0:T(256)S(1)} %iota_add_fusion, f32[]{:T(128)S(6)} %neg.22), kind=kOutput, calls=%fused_computation.23 | convolution fusion | flops 2422210560 | bytes 6489100 | tf_op jit(solution)/shard_map/dot_general | solution.py:51
  122.1 0.0 collective-permute-done.1
  122.1 0.0 copy-done
  122.1 3.2 %convolution_add_fusion = f32[256,1152]{1,0:T(8,128)} fusion(f32[256,1152]{1,0:T(8,128)} %fusion.17, bf16[256,1152]{1,0:T(8,128)(2,1)S(1)} %collective-permute-done.1, bf16[256,1152]{1,0:T(8,128)(2,1)S(1)} %copy-done, f32[]{:T(128)} %bitcast.22, f32[]{:T(128)} %bitcast.18, f32[]{:T(128)S(6)} %mul.64), kind=kOutput, calls=%fused_computation | convolution fusion | flops 302743552 | bytes 3538956 | tf_op jit(solution)/shard_map/dot_general | solution.py:67
  125.4 0.0 collective-permute-done
  125.4 1.9 %convolution_add_fusion.1 = f32[256,1152]{1,0:T(8,128)} fusion(f32[256,1152]{1,0:T(8,128)S(1)} %fusion.16, bf16[256,1152]{1,0:T(8,128)(2,1)S(1)} %collective-permute-done, bf16[256,1152]{1,0:T(8,128)(2,1)S(1)} %copy-done.1, f32[]{:T(128)} %bitcast.20, f32[]{:T(128)} %bitcast.16, f32[]{:T(128)S(6)} %mul.64), kind=kOutput, calls=%fused_computation.1 | convolution fusion | flops 302743552 | bytes 3538956 | tf_op jit(solution)/shard_map/dot_general | solution.py:39
  (1 shorter events, 0.0 us)
Async XLA Ops:
  7.2 56.4 %all-gather.5.cloned.1.call-start = ((), (), s32[]{:S(2)}) async-start(), calls=%async_computation.1 | async-start | bytes 5308416 | tf_op jit(solution)/shard_map/all_gather | solution.py:42
  7.9 107.3 %all-gather.3.cloned.1.call-start = ((), (), s32[]{:S(2)}) async-start(), calls=%async_computation | async-start | bytes 5308416 | tf_op jit(solution)/shard_map/all_gather | solution.py:41
  8.6 113.5 %collective-permute-start.1 = (bf16[256,1152]{1,0:T(8,128)(2,1)}, bf16[256,1152]{1,0:T(8,128)(2,1)S(1)}, u32[]{:S(2)}, u32[]{:S(2)}) collective-permute-start(bf16[256,1152]{1,0:T(8,128)(2,1)} %param.4), channel_id=1, source_target_pairs={{0,24},{8,0},{16,8},{24,16},{1,25},{9,1},{17,9},{25,17},{2,26},{10... | collective-permute-start | bytes 1769480 | tf_op jit(solution)/shard_map/ppermute | solution.py:9
  12.6 112.7 %collective-permute-start = (bf16[256,1152]{1,0:T(8,128)(2,1)}, bf16[256,1152]{1,0:T(8,128)(2,1)S(1)}, u32[]{:S(2)}, u32[]{:S(2)}) collective-permute-start(bf16[256,1152]{1,0:T(8,128)(2,1)} %param.5), channel_id=1, source_target_pairs={{0,8},{8,16},{16,24},{24,0},{1,9},{9,17},{17,25},{25,1},{2,10},{10... | collective-permute-start | bytes 1769480 | tf_op jit(solution)/shard_map/ppermute | solution.py:9
  63.6 51.6 %copy-start.1 = (bf16[256,1152]{1,0:T(8,128)(2,1)S(1)}, bf16[256,1152]{1,0:T(8,128)(2,1)}, u32[]{:S(2)}) copy-start(bf16[256,1152]{1,0:T(8,128)(2,1)} %param.4) | copy-start | bytes 1769476
  115.2 6.9 %copy-start = (bf16[256,1152]{1,0:T(8,128)(2,1)S(1)}, bf16[256,1152]{1,0:T(8,128)(2,1)}, u32[]{:S(2)}) copy-start(bf16[256,1152]{1,0:T(8,128)(2,1)} %param.5) | copy-start | bytes 1769476
Sparse Core Ops, SparseCore 0:
  9.6 53.9 all-gather.4
  65.2 49.9 all-gather.2
where the time goes:
time: 134 us
  waiting for transfers between devices  94.6 us (71%)
  matrix products  20.1 us (15%)
  between operations  15.4 us (11%)
  starting transfers between devices  4.05 us (3%)
    all_gather x1, waiting for transfers between devices, shards(): lax.all_gather(picture_embedding_matrix, 'member', axis=0, tiled=True)  49.6 us
    all_gather x1, waiting for transfers between devices, shards(): lax.all_gather(caption_embedding_matrix, 'member', axis=0, tiled=True)  43.6 us
    dot_general x1, matrix products, shards(): jnp.dot(text_coeffs, group_img, preferred_element_type=jnp.float32)  8.07 us
    dot_general x1, matrix products, shards(): jnp.dot(score_multipliers, group_text_rows, preferred_element_type=jnp.fl...  6.88 us
    ppermute x2, starting transfers between devices, passed_along(): lax.ppermute(shard, axis, [(i, (i + by) % devices) for i in range(devices)])  3.98 us
    dot_general x1, matrix products, shards(): jnp.dot(next_coeffs, img_next, preferred_element_type=jnp.float32)  3.22 us
  transfers between devices with their start and end apart: 4, of which 2 were waited for; matrix products, arithmetic and copies ran while one was open for 14% of the time, Pallas kernels for 0%

commit v1 on v0

v1 whole, which is shorter than its diff:
```python
import functools

import jax
import jax.numpy as jnp
from jax import lax
from jax.experimental import pallas as pl
from jax.experimental.pallas import tpu as pltpu
from jax.sharding import PartitionSpec as P

MESH = pl.DeviceIdType.MESH
F32 = jnp.float32
PIECES = 4


def contract(a, b, da, db):
    return lax.dot_general(a, b, (((da,), (db,)), ((), ())), preferred_element_type=F32)


def kernel(
    groups, n, sharp_ref, bias_ref, img_ref, txt_ref, gi_ref, gt_ref,
    other, gi_other, gi_in, txt_prev, img_next, tbuf, coef, gin, gout, vin, vout,
    t_send, t_recv, g_send, g_recv, v_send, v_recv, x_send, x_recv,
):
    rows, width = img_ref.shape
    piece = rows // PIECES
    group = lax.axis_index("group")
    member = lax.axis_index("member")
    chip, core = member // 2, member % 2
    partner = (group, member + 1 - 2 * core)
    ahead = ((group + 1) % groups, member)
    behind = ((group + groups - 1) % groups, member)
    right, left = (group, member + 2), (group, member - 2)
    has_right, has_left = chip + 1 < n, chip > 0
    sharp, bias = sharp_ref[0], bias_ref[0]

    barrier = pltpu.get_barrier_semaphore()
    for device in (partner, ahead, behind):
        pl.semaphore_signal(barrier, inc=1, device_id=device, device_id_type=MESH)
    for exists, device in ((has_right, right), (has_left, left)):
        @pl.when(exists)
        def _():
            pl.semaphore_signal(barrier, inc=1, device_id=device, device_id_type=MESH)
    pl.semaphore_wait(barrier, 3 + has_right.astype(jnp.int32) + has_left.astype(jnp.int32))

    def remote(src, dst, send, recv, device):
        return pltpu.make_async_remote_copy(
            src_ref=src, dst_ref=dst, send_sem=send, recv_sem=recv,
            device_id=device, device_id_type=MESH,
        )

    def own_text(slot, device):
        return remote(txt_ref, tbuf.at[chip], t_send.at[slot], t_recv.at[chip], device)

    def passed_text(b, device):
        return remote(tbuf.at[b], tbuf.at[b], t_send.at[b], t_recv.at[b], device)

    def sums(b, slot, p, device):
        return remote(gout.at[b, p], gin.at[slot, p], g_send.at[b, p], g_recv.at[slot, p], device)

    def means(b, slot, p, device):
        return remote(vout.at[b, p], vin.at[slot, p], v_send.at[b, p], v_recv.at[slot, p], device)

    swap = remote(img_ref, other, x_send.at[0], x_recv.at[0], partner)
    to_ahead = remote(txt_ref, txt_prev, x_send.at[1], x_recv.at[1], ahead)
    to_behind = remote(img_ref, img_next, x_send.at[2], x_recv.at[2], behind)
    give = remote(gi_other, gi_in, x_send.at[3], x_recv.at[3], partner)

    swap.start()

    @pl.when(has_right)
    def _():
        own_text(chip, right).start()

    @pl.when(has_left)
    def _():
        own_text(n, left).start()

    to_ahead.start()
    to_behind.start()

    def weights(dots, matching):
        logits = sharp * dots + bias
        if matching:
            hit = lax.broadcasted_iota(jnp.int32, dots.shape, 0) == lax.broadcasted_iota(
                jnp.int32, dots.shape, 1
            )
            sign = jnp.where(hit, 1.0, -1.0).astype(F32)
            return (-sign * (sharp / (1.0 + jnp.exp(sign * logits)))).astype(jnp.bfloat16)
        return (sharp / (1.0 + jnp.exp(-logits))).astype(jnp.bfloat16)

    def text_block(block_ref, b):
        for half, img, total in ((0, img_ref, gi_ref), (1, other, gi_other)):
            c = weights(contract(block_ref[...], img[...], 1, 1), False)
            coef[b, half] = c
            total[...] += contract(c, block_ref[...], 0, 0)

    def share(b, p):
        part = pl.ds(pl.multiple_of(p * piece, piece), piece)
        return contract(coef[b, 0, part, :], img_ref[...], 1, 0) + contract(
            coef[b, 1, part, :], other[...], 1, 0
        )

    c = weights(contract(txt_ref[...], img_ref[...], 1, 1), True)
    gi_ref[...] = contract(c, txt_ref[...], 0, 0)
    gt_ref[...] = contract(c, img_ref[...], 1, 0)
    swap.wait()
    c = weights(contract(txt_ref[...], other[...], 1, 1), False)
    gi_other[...] = contract(c, txt_ref[...], 0, 0)
    gt_ref[...] += contract(c, other[...], 1, 0)

    def send_on(b, slot, p, total, mean, device):
        middle = jnp.mean(total, axis=0, keepdims=True)
        gout[b, p] = (total - middle).astype(jnp.bfloat16)
        vout[b, p] = middle if mean is None else middle + mean
        sums(b, slot, p, device).start()
        means(b, slot, p, device).start()

    def arrived(slot, p):
        sums(0, slot, p, partner).wait_recv()
        means(0, slot, p, partner).wait_recv()

    def slot_right(b):
        return jnp.where(chip + 1 == b, n, b)

    def phase(t, carry):
        from_left, from_right = chip - t, chip + t
        for valid, b, more, device in (
            (from_left >= 0, from_left, has_right, right),
            (from_right < n, from_right, has_left, left),
        ):
            @pl.when(valid)
            def _():
                passed_text(b, partner).wait_recv()

                @pl.when(more)
                def _():
                    passed_text(b, device).start()

        for valid, b in ((from_left >= 0, from_left), (from_right < n, from_right)):
            @pl.when(valid)
            def _():
                text_block(tbuf.at[b], b)

        low, high = n - 1 - t, t

        @pl.when(jnp.logical_not(has_right))
        def _():
            @pl.loop(0, PIECES)
            def _(p):
                send_on(low, low, p, share(low, p), None, left)

        @pl.when(jnp.logical_not(has_left))
        def _():
            @pl.loop(0, PIECES)
            def _(p):
                send_on(high, slot_right(high), p, share(high, p), None, right)

        @pl.when(t == n - 1)
        def _():
            give.start()
            to_ahead.wait_recv()
            c = weights(contract(img_ref[...], txt_prev[...], 1, 1), False)
            gi_ref[...] += contract(c, txt_prev[...], 1, 0)
            to_behind.wait_recv()
            c = weights(contract(txt_ref[...], img_next[...], 1, 1), False)
            gt_ref[...] += contract(c, img_next[...], 1, 0)

        @pl.loop(0, PIECES)
        def _(p):
            @pl.when((low < chip) & has_right)
            def _():
                here = share(low, p)
                arrived(low, p)
                send_on(low, low, p, here + gin[low, p].astype(F32), vin[low, p], left)

            @pl.when((high > chip) & has_left)
            def _():
                here = share(high, p)
                arrived(high, p)
                send_on(
                    high, slot_right(high), p, here + gin[high, p].astype(F32), vin[high, p], right
                )

        for owner, slot in ((low == chip, chip), (high == chip, n)):
            @pl.when(owner)
            def _():
                @pl.loop(0, PIECES)
                def _(p):
                    arrived(slot, p)
                    part = pl.ds(pl.multiple_of(p * piece, piece), piece)
                    gt_ref[part, :] += gin[slot, p].astype(F32) + vin[slot, p]

        return carry

    lax.fori_loop(1, n, phase, 0)

    give.wait_recv()
    gi_ref[...] += gi_in[...]

    give.wait_send()
    to_ahead.wait_send()
    to_behind.wait_send()

    @pl.when(has_right)
    def _():
        own_text(chip, right).wait_send()

    @pl.when(has_left)
    def _():
        own_text(n, left).wait_send()

    @pl.loop(0, n)
    def _(b):
        @pl.when(((b < chip) & has_right) | ((b > chip) & has_left))
        def _():
            passed_text(b, partner).wait_send()

        @pl.when(b != chip)
        def _():
            @pl.loop(0, PIECES)
            def _(p):
                sums(b, b, p, partner).wait_send()
                means(b, b, p, partner).wait_send()


def solution(mesh):
    groups, members = mesh.shape["group"], mesh.shape["member"]
    n = members // 2

    def shards(images, texts, sharpness, offset):
        rows, width = images.shape
        piece = rows // PIECES
        bf16 = jnp.bfloat16
        out = jax.ShapeDtypeStruct((rows, width), F32)
        vmem = pl.BlockSpec(memory_space=pltpu.VMEM)
        smem = pl.BlockSpec(memory_space=pltpu.SMEM)
        dma = pltpu.SemaphoreType.DMA
        return pl.pallas_call(
            functools.partial(kernel, groups, n),
            out_shape=(out, out),
            in_specs=[smem, smem, vmem, vmem],
            out_specs=(vmem, vmem),
            scratch_shapes=[
                pltpu.VMEM((rows, width), bf16),
                pltpu.VMEM((rows, width), F32),
                pltpu.VMEM((rows, width), F32),
                pltpu.VMEM((rows, width), bf16),
                pltpu.VMEM((rows, width), bf16),
                pltpu.VMEM((n, rows, width), bf16),
                pltpu.VMEM((n, 2, rows, rows), bf16),
                pltpu.VMEM((n + 1, PIECES, piece, width), bf16),
                pltpu.VMEM((n, PIECES, piece, width), bf16),
                pltpu.VMEM((n + 1, PIECES, 1, width), F32),
                pltpu.VMEM((n, PIECES, 1, width), F32),
                dma((n + 1,)),
                dma((n,)),
                dma((n, PIECES)),
                dma((n + 1, PIECES)),
                dma((n, PIECES)),
                dma((n + 1, PIECES)),
                dma((4,)),
                dma((4,)),
            ],
            compiler_params=pltpu.CompilerParams(
                collective_id=0, has_side_effects=True, vmem_limit_bytes=60 * 1024 * 1024
            ),
        )(sharpness, offset, images, texts)

    spec = P(("group", "member"), None)
    return jax.shard_map(
        shards, mesh=mesh, in_specs=(spec, spec, P(), P()), out_specs=(spec, spec), check_vma=False
    )
```

time: 134 us -> 106 us (0.79); the launches traced: 134 us -> 104 us
  Pallas kernels: 0 us -> 98.8 us
  waiting for transfers between devices: 94.6 us -> 0 us
  matrix products: 20.1 us -> 0 us
  between operations: 15.4 us -> 1.94 us
  starting transfers between devices: 4.05 us -> 0 us
  local copies, waits for them, and re-layouts: 0.01 us -> 3.47 us
    pallas_call x0 -> x1, Pallas kernels: none -> 98.8 us  [shards(): pl.pallas_call(functools.partial(kernel, groups, n), out_shape=(out, out)...]
    all_gather x2 -> x0, waiting for transfers between devices: 93.2 us -> none  [the longest x1 49.6 us: shards(): lax.all_gather(picture_embedding_matrix, 'member', axis=0, tiled=True)]
    dot_general x4 -> x0, matrix products: 20.1 us -> none  [the longest x1 8.07 us: shards(): jnp.dot(text_coeffs, group_img, preferred_element_type=jnp.float32)]
    ppermute x2 -> x0, starting transfers between devices: 3.98 us -> none  [passed_along(): lax.ppermute(shard, axis, [(i, (i + by) % devices) for i in range(devices)])]
    unnamed x4, local copies, waits for them, and re-layouts: 0.01 us -> 3.47 us
    unnamed x2 -> x0, waiting for transfers between devices: 1.38 us -> none
  transfers between devices with their start and end apart: 4 -> 0, of which waited for: 2 -> 0; matrix products, arithmetic and copies ran while one was open for 14% -> 0% of each run, Pallas kernels for 0% -> 0%
where the time goes in v1:
time: 106 us; the launch traced here: 104 us
  Pallas kernels  98.8 us (93%)
  local copies, waits for them, and re-layouts  3.47 us (3%)
  between operations  1.94 us (2%)
    pallas_call x1, Pallas kernels, shards(): pl.pallas_call(functools.partial(kernel, groups, n), out_shape=(out, out)...  98.8 us
    unnamed x4, local copies, waits for them, and re-layouts  3.47 us

profile of v1, /device:TPU:0, one launch (start us, length us, event | category | flops | bytes accessed | tf_op | source)
XLA Modules:
  0.0 104.2 jit_solution(6651249731999555441)
XLA Ops:
  1.9 98.8 %shard_map.59 = (f32[256,1152]{1,0:T(8,128)}, f32[256,1152]{1,0:T(8,128)}) custom-call(f32[1]{0:T(128)S(6)} %copy.8.sharp_ref, f32[1]{0:T(128)S(6)} %copy.9.bias_ref, bf16[256,1152]{1,0:T(8,128)(2,1)} %img_ref.1, bf16[256,1152]{1,0:T(8,128)(2,1)} %txt_ref.1), custom_call_target="tpu_custom_call" | custom-call | tf_op jit(solution)/shard_map/pallas_call | solution.py:238
  100.7 0.0 copy-start
  100.7 2.5 %copy.10 = f32[256,1152]{1,0:T(8,128)} copy(f32[256,1152]{1,0:T(8,128)} %get-tuple-element.4) | data formatting | bytes 2359296
  103.1 0.0 copy-done
  103.1 1.0 copy.11
Async XLA Ops:
  100.7 2.5 %copy-start = (f32[256,1152]{1,0:T(8,128)S(1)}, f32[256,1152]{1,0:T(8,128)}, u32[]{:S(2)}) copy-start(f32[256,1152]{1,0:T(8,128)} %get-tuple-element.5) | copy-start | bytes 3538948

commit v2 on v1

--- a/solution.py
+++ b/solution.py
@@ -10,6 +10,7 @@
 MESH = pl.DeviceIdType.MESH
 F32 = jnp.float32
 PIECES = 4
+SKEW = 2
 
 
 def contract(a, b, da, db):
@@ -48,11 +49,18 @@
             device_id=device, device_id_type=MESH,
         )
 
-    def own_text(slot, device):
-        return remote(txt_ref, tbuf.at[chip], t_send.at[slot], t_recv.at[chip], device)
-
-    def passed_text(b, device):
-        return remote(tbuf.at[b], tbuf.at[b], t_send.at[b], t_recv.at[b], device)
+    def part_of(p):
+        return pl.ds(pl.multiple_of(p * piece, piece), piece)
+
+    def own_text(slot, p, device):
+        return remote(
+            txt_ref.at[part_of(p)], tbuf.at[chip, part_of(p)],
+            t_send.at[slot, p], t_recv.at[chip, p], device,
+        )
+
+    def passed_text(b, p, device):
+        block = tbuf.at[b, part_of(p)]
+        return remote(block, block, t_send.at[b, p], t_recv.at[b, p], device)
 
     def sums(b, slot, p, device):
         return remote(gout.at[b, p], gin.at[slot, p], g_send.at[b, p], g_recv.at[slot, p], device)
@@ -67,13 +75,14 @@
 
     swap.start()
 
-    @pl.when(has_right)
-    def _():
-        own_text(chip, right).start()
-
-    @pl.when(has_left)
-    def _():
-        own_text(n, left).start()
+    for p in range(PIECES):
+        @pl.when(has_right)
+        def _():
+            own_text(chip, p, right).start()
+
+        @pl.when(has_left)
+        def _():
+            own_text(n, p, left).start()
 
     to_ahead.start()
     to_behind.start()
@@ -88,14 +97,16 @@
             return (-sign * (sharp / (1.0 + jnp.exp(sign * logits)))).astype(jnp.bfloat16)
         return (sharp / (1.0 + jnp.exp(-logits))).astype(jnp.bfloat16)
 
-    def text_block(block_ref, b):
-        for half, img, total in ((0, img_ref, gi_ref), (1, other, gi_other)):
-            c = weights(contract(block_ref[...], img[...], 1, 1), False)
-            coef[b, half] = c
-            total[...] += contract(c, block_ref[...], 0, 0)
+    def weigh(b, part):
+        for half, img in ((0, img_ref), (1, other)):
+            coef[b, half, part, :] = weights(contract(tbuf[b, part, :], img[...], 1, 1), False)
+
+    def add_images(b):
+        for half, total in ((0, gi_ref), (1, gi_other)):
+            total[...] += contract(coef[b, half], tbuf[b], 0, 0)
 
     def share(b, p):
-        part = pl.ds(pl.multiple_of(p * piece, piece), piece)
+        part = part_of(p)
         return contract(coef[b, 0, part, :], img_ref[...], 1, 0) + contract(
             coef[b, 1, part, :], other[...], 1, 0
         )
@@ -122,38 +133,51 @@
     def slot_right(b):
         return jnp.where(chip + 1 == b, n, b)
 
+    def collect(low, high):
+        for owner, slot in ((low == chip, chip), (high == chip, n)):
+            @pl.when(owner)
+            def _():
+                @pl.loop(0, PIECES)
+                def _(p):
+                    arrived(slot, p)
+                    gt_ref[part_of(p), :] += gin[slot, p].astype(F32) + vin[slot, p]
+
     def phase(t, carry):
         from_left, from_right = chip - t, chip + t
-        for valid, b, more, device in (
-            (from_left >= 0, from_left, has_right, right),
-            (from_right < n, from_right, has_left, left),
-        ):
+        low, high = n - 1 - t, t
+        sides = (
+            (from_left >= 0, from_left, has_right, right, left, from_left),
+            (from_right < n, from_right, has_left, left, right, slot_right(from_right)),
+        )
+
+        @pl.loop(0, PIECES)
+        def _(p):
+            for valid, b, more, onward, back, slot in sides:
+                @pl.when(valid)
+                def _():
+                    passed_text(b, p, partner).wait_recv()
+
+                    @pl.when(more)
+                    def _():
+                        passed_text(b, p, onward).start()
+
+                    @pl.when(jnp.logical_not(more))
+                    def _():
+                        weigh(b, part_of(p))
+                        send_on(b, slot, p, share(b, p), None, back)
+
+        for valid, b, more, onward, back, slot in sides:
             @pl.when(valid)
             def _():
-                passed_text(b, partner).wait_recv()
-
                 @pl.when(more)
                 def _():
-                    passed_text(b, device).start()
-
-        for valid, b in ((from_left >= 0, from_left), (from_right < n, from_right)):
-            @pl.when(valid)
-            def _():
-                text_block(tbuf.at[b], b)
-
-        low, high = n - 1 - t, t
-
-        @pl.when(jnp.logical_not(has_right))
-        def _():
-            @pl.loop(0, PIECES)
-            def _(p):
-                send_on(low, low, p, share(low, p), None, left)
-
-        @pl.when(jnp.logical_not(has_left))
-        def _():
-            @pl.loop(0, PIECES)
-            def _(p):
-                send_on(high, slot_right(high), p, share(high, p), None, right)
+                    weigh(b, pl.ds(0, rows))
+
+                add_images(b)
+
+        @pl.when(t >= 2)
+        def _():
+            collect(low + 1, high - 1)
 
         @pl.when(t == n - 1)
         def _():
@@ -165,34 +189,30 @@
             c = weights(contract(txt_ref[...], img_next[...], 1, 1), False)
             gt_ref[...] += contract(c, img_next[...], 1, 0)
 
-        @pl.loop(0, PIECES)
-        def _(p):
-            @pl.when((low < chip) & has_right)
-            def _():
-                here = share(low, p)
-                arrived(low, p)
-                send_on(low, low, p, here + gin[low, p].astype(F32), vin[low, p], left)
-
-            @pl.when((high > chip) & has_left)
-            def _():
-                here = share(high, p)
-                arrived(high, p)
-                send_on(
-                    high, slot_right(high), p, here + gin[high, p].astype(F32), vin[high, p], right
-                )
-
-        for owner, slot in ((low == chip, chip), (high == chip, n)):
-            @pl.when(owner)
-            def _():
-                @pl.loop(0, PIECES)
-                def _(p):
-                    arrived(slot, p)
-                    part = pl.ds(pl.multiple_of(p * piece, piece), piece)
-                    gt_ref[part, :] += gin[slot, p].astype(F32) + vin[slot, p]
+        @pl.when(has_left & has_right & ((low < chip) | (high > chip)))
+        def _():
+            @pl.loop(0, PIECES + SKEW * (n - 1))
+            def _(step):
+                p_low, p_high = step - SKEW * (n - 1 - chip), step - SKEW * chip
+
+                @pl.when((low < chip) & (p_low >= 0) & (p_low < PIECES))
+                def _():
+                    here = share(low, p_low)
+                    arrived(low, p_low)
+                    total = here + gin[low, p_low].astype(F32)
+                    send_on(low, low, p_low, total, vin[low, p_low], left)
+
+                @pl.when((high > chip) & (p_high >= 0) & (p_high < PIECES))
+                def _():
+                    here = share(high, p_high)
+                    arrived(high, p_high)
+                    total = here + gin[high, p_high].astype(F32)
+                    send_on(high, slot_right(high), p_high, total, vin[high, p_high], right)
 
         return carry
 
     lax.fori_loop(1, n, phase, 0)
+    collect(0, n - 1)
 
     give.wait_recv()
     gi_ref[...] += gi_in[...]
@@ -201,24 +221,24 @@
     to_ahead.wait_send()
     to_behind.wait_send()
 
-    @pl.when(has_right)
-    def _():
-        own_text(chip, right).wait_send()
-
-    @pl.when(has_left)
-    def _():
-        own_text(n, left).wait_send()
-
-    @pl.loop(0, n)
-    def _(b):
-        @pl.when(((b < chip) & has_right) | ((b > chip) & has_left))
-        def _():
-            passed_text(b, partner).wait_send()
-
-        @pl.when(b != chip)
-        def _():
-            @pl.loop(0, PIECES)
-            def _(p):
+    @pl.loop(0, PIECES)
+    def _(p):
+        @pl.when(has_right)
+        def _():
+            own_text(chip, p, right).wait_send()
+
+        @pl.when(has_left)
+        def _():
+            own_text(n, p, left).wait_send()
+
+        @pl.loop(0, n)
+        def _(b):
+            @pl.when(((b < chip) & has_right) | ((b > chip) & has_left))
+            def _():
+                passed_text(b, p, partner).wait_send()
+
+            @pl.when(b != chip)
+            def _():
                 sums(b, b, p, partner).wait_send()
                 means(b, b, p, partner).wait_send()
 
@@ -252,8 +272,8 @@
                 pltpu.VMEM((n, PIECES, piece, width), bf16),
                 pltpu.VMEM((n + 1, PIECES, 1, width), F32),
                 pltpu.VMEM((n, PIECES, 1, width), F32),
-                dma((n + 1,)),
-                dma((n,)),
+                dma((n + 1, PIECES)),
+                dma((n, PIECES)),
                 dma((n, PIECES)),
                 dma((n + 1, PIECES)),
                 dma((n, PIECES)),

time: 106 us -> 79.6 us (0.75); the launches traced: 104 us -> 79.4 us
  Pallas kernels: 98.8 us -> 74 us
    pallas_call x1, Pallas kernels: 98.8 us -> 74 us  [shards(): pl.pallas_call(functools.partial(kernel, groups, n), out_shape=(out, out)...]
where the time goes in v2:
time: 79.6 us; the launch traced here: 79.4 us
  Pallas kernels  74 us (93%)
  local copies, waits for them, and re-layouts  3.47 us (4%)
  between operations  1.94 us (2%)
    pallas_call x1, Pallas kernels, shards(): pl.pallas_call(functools.partial(kernel, groups, n), out_shape=(out, out)...  74 us
    unnamed x4, local copies, waits for them, and re-layouts  3.47 us

profile of v2, /device:TPU:0, one launch (start us, length us, event | category | flops | bytes accessed | tf_op | source)
XLA Modules:
  0.0 79.4 jit_solution(1867639955433056300)
XLA Ops:
  1.9 74.0 %shard_map.59 = (f32[256,1152]{1,0:T(8,128)}, f32[256,1152]{1,0:T(8,128)}) custom-call(f32[1]{0:T(128)S(6)} %copy.8.sharp_ref, f32[1]{0:T(128)S(6)} %copy.9.bias_ref, bf16[256,1152]{1,0:T(8,128)(2,1)} %img_ref.1, bf16[256,1152]{1,0:T(8,128)(2,1)} %txt_ref.1), custom_call_target="tpu_custom_call" | custom-call | tf_op jit(solution)/shard_map/pallas_call | solution.py:258
  76.0 0.0 copy-start
  76.0 2.5 %copy.10 = f32[256,1152]{1,0:T(8,128)} copy(f32[256,1152]{1,0:T(8,128)} %get-tuple-element.4) | data formatting | bytes 2359296
  78.4 0.0 copy-done
  78.4 1.0 %copy.11 = f32[256,1152]{1,0:T(8,128)} copy(f32[256,1152]{1,0:T(8,128)S(1)} %copy-done) | data formatting | bytes 2359296
Async XLA Ops:
  76.0 2.5 %copy-start = (f32[256,1152]{1,0:T(8,128)S(1)}, f32[256,1152]{1,0:T(8,128)}, u32[]{:S(2)}) copy-start(f32[256,1152]{1,0:T(8,128)} %get-tuple-element.5) | copy-start | bytes 3538948

commit v3 on v2

--- a/solution.py
+++ b/solution.py
@@ -11,6 +11,7 @@
 F32 = jnp.float32
 PIECES = 4
 SKEW = 2
+EARLY = 2
 
 
 def contract(a, b, da, db):
@@ -133,15 +134,6 @@
     def slot_right(b):
         return jnp.where(chip + 1 == b, n, b)
 
-    def collect(low, high):
-        for owner, slot in ((low == chip, chip), (high == chip, n)):
-            @pl.when(owner)
-            def _():
-                @pl.loop(0, PIECES)
-                def _(p):
-                    arrived(slot, p)
-                    gt_ref[part_of(p), :] += gin[slot, p].astype(F32) + vin[slot, p]
-
     def phase(t, carry):
         from_left, from_right = chip - t, chip + t
         low, high = n - 1 - t, t
@@ -164,7 +156,20 @@
                     @pl.when(jnp.logical_not(more))
                     def _():
                         weigh(b, part_of(p))
-                        send_on(b, slot, p, share(b, p), None, back)
+
+                        @pl.when((t > 1) | (p < EARLY))
+                        def _():
+                            send_on(b, slot, p, share(b, p), None, back)
+
+        for more, b, slot, back in (
+            (has_right, chip - 1, chip - 1, left),
+            (has_left, chip + 1, n, right),
+        ):
+            @pl.when((t == n - 1) & jnp.logical_not(more))
+            def _():
+                @pl.loop(EARLY, PIECES)
+                def _(p):
+                    send_on(b, slot, p, share(b, p), None, back)
 
         for valid, b, more, onward, back, slot in sides:
             @pl.when(valid)
@@ -175,19 +180,9 @@
 
                 add_images(b)
 
-        @pl.when(t >= 2)
-        def _():
-            collect(low + 1, high - 1)
-
         @pl.when(t == n - 1)
         def _():
             give.start()
-            to_ahead.wait_recv()
-            c = weights(contract(img_ref[...], txt_prev[...], 1, 1), False)
-            gi_ref[...] += contract(c, txt_prev[...], 1, 0)
-            to_behind.wait_recv()
-            c = weights(contract(txt_ref[...], img_next[...], 1, 1), False)
-            gt_ref[...] += contract(c, img_next[...], 1, 0)
 
         @pl.when(has_left & has_right & ((low < chip) | (high > chip)))
         def _():
@@ -212,10 +207,23 @@
         return carry
 
     lax.fori_loop(1, n, phase, 0)
-    collect(0, n - 1)
-
+
+    to_ahead.wait_recv()
+    c = weights(contract(img_ref[...], txt_prev[...], 1, 1), False)
+    gi_ref[...] += contract(c, txt_prev[...], 1, 0)
+    to_behind.wait_recv()
+    c = weights(contract(txt_ref[...], img_next[...], 1, 1), False)
+    gt_ref[...] += contract(c, img_next[...], 1, 0)
     give.wait_recv()
     gi_ref[...] += gi_in[...]
+
+    for exists, slot in ((has_left, n), (has_right, chip)):
+        @pl.when(exists)
+        def _():
+            @pl.loop(0, PIECES)
+            def _(p):
+                arrived(slot, p)
+                gt_ref[part_of(p), :] += gin[slot, p].astype(F32) + vin[slot, p]
 
     give.wait_send()
     to_ahead.wait_send()

time: 79.6 us -> 74.5 us (0.936)
  Pallas kernels: 74 us -> 68.9 us
    pallas_call x1, Pallas kernels: 74 us -> 68.9 us  [shards(): pl.pallas_call(functools.partial(kernel, groups, n), out_shape=(out, out)...]
where the time goes in v3:
time: 74.5 us; the launch traced here: 74.3 us
  Pallas kernels  68.9 us (92%)
  local copies, waits for them, and re-layouts  3.47 us (5%)
  between operations  1.94 us (3%)
    pallas_call x1, Pallas kernels, shards(): pl.pallas_call(functools.partial(kernel, groups, n), out_shape=(out, out)...  68.9 us
    unnamed x4, local copies, waits for them, and re-layouts  3.47 us

profile of v3, /device:TPU:0, one launch (start us, length us, event | category | flops | bytes accessed | tf_op | source)
XLA Modules:
  0.0 74.3 jit_solution(17991452956205152169)
XLA Ops:
  1.9 68.9 %shard_map.59 = (f32[256,1152]{1,0:T(8,128)}, f32[256,1152]{1,0:T(8,128)}) custom-call(f32[1]{0:T(128)S(6)} %copy.8.sharp_ref, f32[1]{0:T(128)S(6)} %copy.9.bias_ref, bf16[256,1152]{1,0:T(8,128)(2,1)} %img_ref.1, bf16[256,1152]{1,0:T(8,128)(2,1)} %txt_ref.1), custom_call_target="tpu_custom_call" | custom-call | tf_op jit(solution)/shard_map/pallas_call | solution.py:266
  70.8 0.0 copy-start
  70.8 2.5 %copy.10 = f32[256,1152]{1,0:T(8,128)} copy(f32[256,1152]{1,0:T(8,128)} %get-tuple-element.4) | data formatting | bytes 2359296
  73.3 0.0 copy-done
  73.3 1.0 %copy.11 = f32[256,1152]{1,0:T(8,128)} copy(f32[256,1152]{1,0:T(8,128)S(1)} %copy-done) | data formatting | bytes 2359296
Async XLA Ops:
  70.8 2.5 %copy-start = (f32[256,1152]{1,0:T(8,128)S(1)}, f32[256,1152]{1,0:T(8,128)}, u32[]{:S(2)}) copy-start(f32[256,1152]{1,0:T(8,128)} %get-tuple-element.5) | copy-start | bytes 3538948

commit v4 on v3

--- a/solution.py
+++ b/solution.py
@@ -290,7 +290,7 @@
                 dma((4,)),
             ],
             compiler_params=pltpu.CompilerParams(
-                collective_id=0, has_side_effects=True, vmem_limit_bytes=60 * 1024 * 1024
+                collective_id=0, has_side_effects=True, vmem_limit_bytes=min(60, 16 + 3 * n) * 1024 * 1024
             ),
         )(sharpness, offset, images, texts)
 

time: 74.5 us -> 72.5 us (0.973)
  Pallas kernels: 68.9 us -> 66.2 us
    pallas_call x1, Pallas kernels: 68.9 us -> 66.2 us  [shards(): pl.pallas_call(functools.partial(kernel, groups, n), out_shape=(out, out)...]
    unnamed x4 -> x6, local copies, waits for them, and re-layouts: 3.47 us -> 4.15 us
where the time goes in v4:
time: 72.5 us; the launch traced here: 72.3 us
  Pallas kernels  66.2 us (91%)
  local copies, waits for them, and re-layouts  4.15 us (6%)
  between operations  1.94 us (3%)
    pallas_call x1, Pallas kernels, shards(): pl.pallas_call(functools.partial(kernel, groups, n), out_shape=(out, out)...  66.2 us
    unnamed x6, local copies, waits for them, and re-layouts  4.15 us

profile of v4, /device:TPU:0, one launch (start us, length us, event | category | flops | bytes accessed | tf_op | source)
XLA Modules:
  0.0 72.3 jit_solution(7625207139613978939)
XLA Ops:
  1.9 0.0 copy-start
  1.9 1.1 %copy-done = bf16[256,1152]{1,0:T(8,128)(2,1)S(1)} copy-done((bf16[256,1152]{1,0:T(8,128)(2,1)S(1)}, bf16[256,1152]{1,0:T(8,128)(2,1)}, u32[]{:S(2)}) %copy-start) | copy-done | bytes 589848
  3.0 0.0 copy-start.1
  3.0 1.1 %copy-done.1 = bf16[256,1152]{1,0:T(8,128)(2,1)S(1)} copy-done((bf16[256,1152]{1,0:T(8,128)(2,1)S(1)}, bf16[256,1152]{1,0:T(8,128)(2,1)}, u32[]{:S(2)}) %copy-start.1) | copy-done | bytes 589848
  4.1 66.2 %shard_map.59 = (f32[256,1152]{1,0:T(8,128)S(1)}, f32[256,1152]{1,0:T(8,128)S(1)}) custom-call(f32[1]{0:T(128)S(6)} %copy.8.sharp_ref, f32[1]{0:T(128)S(6)} %copy.9.bias_ref, bf16[256,1152]{1,0:T(8,128)(2,1)S(1)} %copy-done, bf16[256,1152]{1,0:T(8,128)(2,1)S(1)} %copy-done.1), custom_call_target="tpu_custom_call" | custom-call | tf_op jit(solution)/shard_map/pallas_call | solution.py:266
  70.2 1.0 %copy.10 = f32[256,1152]{1,0:T(8,128)} copy(f32[256,1152]{1,0:T(8,128)S(1)} %get-tuple-element.4) | data formatting | bytes 2359296
  71.3 1.0 %copy.11 = f32[256,1152]{1,0:T(8,128)} copy(f32[256,1152]{1,0:T(8,128)S(1)} %get-tuple-element.5) | data formatting | bytes 2359296
Async XLA Ops:
  1.9 1.1 %copy-start = (bf16[256,1152]{1,0:T(8,128)(2,1)S(1)}, bf16[256,1152]{1,0:T(8,128)(2,1)}, u32[]{:S(2)}) copy-start(bf16[256,1152]{1,0:T(8,128)(2,1)} %img_ref.1) | copy-start | bytes 1769476
  3.0 1.1 %copy-start.1 = (bf16[256,1152]{1,0:T(8,128)(2,1)S(1)}, bf16[256,1152]{1,0:T(8,128)(2,1)}, u32[]{:S(2)}) copy-start(bf16[256,1152]{1,0:T(8,128)(2,1)} %txt_ref.1) | copy-start | bytes 1769476
